TPU v7x, 32 devices: a whole 2x2x4 slice. The times are simulated.
32 devices in a mesh: grp: 4 (over y, core), dev: 8 (over z, x).
Axes of the slice: x: 2, y: 2, z: 4, core: 2. Of those that a mesh axis runs over, the one named last changes fastest.
Arguments:
- matrix: float32 [16384, 128], P(('grp', 'dev')), may hold values from -6 to 6
- flip_bits: int32 [16384], P(('grp', 'dev')), may hold values from 0 to 1
- sample_rows: int32 [2048], replicated, may hold values from 0 to 16383
Outputs:
- sketch: float32 [2048, 128], P(('grp', 'dev'))
- gram: float32 [128, 128], replicated
Inputs may be any that keep to these rules, and one draw needn't show every extreme that they name: `sample_rows`: rows may repeat.
All inputs are finite; a program needn't handle non-finite values.
Results may differ from a plain program's by a relative error of at most 0.000098.
Values sent between devices are 32-bit elements; how exact they have to be, the bound alone decides.
A program may use at most 64 MiB of HBM per device.

v0:
```python
import functools
import math

import jax
import jax.numpy as jnp
from jax import lax
from jax.experimental import pallas as pl
from jax.experimental.pallas import tpu as pltpu
from jax.sharding import PartitionSpec as P

MESH = pl.DeviceIdType.MESH
LANES = 128


def loop(count, fn):
    if count <= 8:
        for step in range(count):
            fn(step)
    else:
        lax.fori_loop(0, count, lambda step, carry: (fn(step), carry)[1], 0)


def parity(bits, width):
    shift = 1
    while shift * 2 < width:
        shift *= 2
    while shift:
        bits = bits ^ (bits >> shift)
        shift //= 2
    return bits & 1


def sign_of(bits, width):
    return (1 - 2 * parity(bits, width)).astype(jnp.float32)


def split3(value):
    high = value.astype(jnp.bfloat16)
    rest = value - high.astype(jnp.float32)
    mid = rest.astype(jnp.bfloat16)
    low = (rest - mid.astype(jnp.float32)).astype(jnp.bfloat16)
    return high, mid, low


def kernel(
    n_grp, n_dev, rows, own,
    x_ref, flip_hbm, sample_hbm, sketch_ref, gram_ref,
    flip_ref, sample_ref, x_full, slabs, flips, cols, index, base, part, blocks, gpart, gslots, gfull, reduced,
    load_sem, pair_send, pair_recv, twin_send, twin_recv, fwd_send, fwd_recv,
    flip_send, flip_recv, rs_send, rs_recv, g_send, g_recv, b_send, b_recv,
    ready,
):
    f32 = jnp.float32
    devices = n_grp * n_dev
    n_y, n_z = n_grp // 2, n_dev // 2
    groups = n_y * n_z
    width = x_ref.shape[1]
    pieces = twin_send.shape[0]
    piece = rows // pieces
    samples = sample_hbm.shape[0] * LANES
    row_bits = rows.bit_length() - 1
    all_bits = (rows * devices).bit_length() - 1
    me_g, me_d = lax.axis_index("grp"), lax.axis_index("dev")
    core, y = lax.rem(me_g, 2), lax.div(me_g, 2)
    x, z = lax.rem(me_d, 2), lax.div(me_d, 2)
    pair_g = me_g + 1 - 2 * core
    twin_d = me_d + 1 - 2 * x
    mine = y * n_z + z

    def remote(src, dst, send, recv, grp, dev):
        return pltpu.make_async_remote_copy(
            src_ref=src, dst_ref=dst, send_sem=send, recv_sem=recv,
            device_id=(grp, dev), device_id_type=MESH,
        )

    barrier = pltpu.get_barrier_semaphore()

    def signal(sem, grp, dev):
        pl.semaphore_signal(sem, inc=1, device_id=(grp, dev), device_id_type=MESH)

    def along_y(step):
        return me_g + 2 * step, me_d

    def along_z(step):
        return me_g, me_d + 2 * step

    def tell_line(sem, at, size, reach, along):
        for step in range(1, min(reach, size - 1) + 1):
            @pl.when(at >= step)
            def _():
                signal(sem, *along(-step))

            @pl.when(at + step < size)
            def _():
                signal(sem, *along(step))

    def line_count(at, size, reach):
        return jnp.minimum(at, reach) + jnp.minimum(size - 1 - at, reach)

    signal(barrier, pair_g, me_d)
    signal(barrier, me_g, twin_d)
    tell_line(barrier, y, n_y, 1, along_y)
    tell_line(barrier, z, n_z, 1, along_z)

    loads = [
        pltpu.make_async_copy(sample_hbm, sample_ref, load_sem.at[0]),
        pltpu.make_async_copy(flip_hbm, flip_ref, load_sem.at[1]),
        pltpu.make_async_copy(x_ref, x_full, load_sem.at[2]),
    ]
    for copy in loads:
        copy.start()
    pl.semaphore_wait(barrier, 2 + line_count(y, n_y, 1) + line_count(z, n_z, 1))

    rounds = []
    for at, size, along in ((z, n_z, along_z), (y, n_y, along_y)):
        reach = 1
        while reach < size - 1:
            rounds.append((at, size, reach, along))
            reach *= 2
    rounds.append((y, n_y, n_y - 1, along_y))

    def open_round(k):
        if k < len(rounds):
            at, size, reach, along = rounds[k]
            tell_line(ready.at[k], at, size, reach, along)
        elif k == len(rounds):
            signal(ready.at[k], me_g, twin_d)
        else:
            signal(ready.at[k], pair_g, me_d)

    def close_round(k):
        if k < len(rounds):
            at, size, reach, along = rounds[k]
            pl.semaphore_wait(ready.at[k], line_count(at, size, reach))
        else:
            pl.semaphore_wait(ready.at[k], 1)

    half = width // 2
    left = lax.broadcasted_iota(jnp.int32, (1, width), 1) < half

    def swap(value):
        return pltpu.roll(value, half, value.ndim - 1)

    for copy in loads:
        copy.wait()
    top, bottom = x_full[pl.ds(0, rows // 2), :], x_full[pl.ds(rows // 2, rows // 2), :]
    slabs[0, 0] = jnp.where(left, top, swap(bottom))
    slabs[1, 0] = jnp.where(left, swap(top), bottom)
    twin, pair = [], []
    for h in range(2):
        for c in range(pieces // 2):
            at = pl.ds(c * piece, piece)
            k = h * (pieces // 2) + c
            copy = remote(
                slabs.at[h, 0, at], slabs.at[h, 2, at],
                twin_send.at[k], twin_recv.at[k], me_g, twin_d,
            )
            copy.start()
            twin.append(copy)
    for h in range(2):
        copy = remote(
            slabs.at[h, 0], slabs.at[h, 1], pair_send.at[h], pair_recv.at[h], pair_g, me_d
        )
        copy.start()
        pair.append(copy)
    flip_copies = [
        remote(flip_ref, flips.at[0], flip_send.at[0], flip_recv.at[0], pair_g, me_d),
        remote(flip_ref, flips.at[1], flip_send.at[1], flip_recv.at[1], me_g, twin_d),
        remote(flips.at[1], flips.at[2], flip_send.at[2], flip_recv.at[2], pair_g, me_d),
    ]
    open_round(0)
    for copy in flip_copies[:2]:
        copy.start()

    span = n_dev * own // LANES
    for i in range(n_y):
        for r in range(span):
            line = sample_ref[pl.ds((i * 2 + core) * span + r, 1), :]
            cols[pl.ds((i * span + r) * LANES, LANES), :] = jnp.transpose(
                jnp.broadcast_to(line, (LANES, LANES))
            )
    for i in range(n_y):
        for j in range(n_z):
            index[pl.ds((i * n_z + j) * own, own), :] = cols[
                pl.ds((i * n_dev + j * 2 + x) * own, own), :
            ]
    close_round(0)
    open_round(1)
    picks = groups * own
    wanted = index[...]
    for k in range(rows // LANES):
        lane = lax.broadcasted_iota(jnp.int32, (picks, LANES), 1) + k * LANES
        base[:, k * LANES:(k + 1) * LANES] = sign_of(wanted & lane, row_bits).astype(jnp.bfloat16)

    owner_signs = [
        sign_of(wanted & ((grp * n_dev + dev) * rows), all_bits)
        for grp, dev in ((me_g, me_d), (pair_g, me_d), (me_g, twin_d), (pair_g, twin_d))
    ]

    def term(h, slot, flip_bits, grp, dev):
        signs = base[...]
        toggles = (1 - 2 * flip_bits).astype(f32).astype(jnp.bfloat16)
        signs = jnp.concatenate(
            [
                signs[:, k * LANES:(k + 1) * LANES] * toggles[k:k + 1, :]
                for k in range(rows // LANES)
            ],
            axis=1,
        )
        packed = slabs[h, slot]
        high, mid, low = split3(packed)
        high_s, mid_s, low_s = split3(swap(packed))
        right = jnp.concatenate(
            [
                jnp.concatenate([jnp.where(left, high, mid_s), low], axis=1),
                jnp.concatenate([jnp.where(left, high_s, mid), low_s], axis=1),
            ],
            axis=0,
        )
        product = jnp.dot(signs, right, preferred_element_type=f32)
        first, last = product[:, :width], product[:, width:]
        return (first + swap(first) + last) * owner_signs[slot]

    def give(h, i, j):
        to_y, to_z = lax.rem(y + i, n_y), lax.rem(z + j, n_z)
        remote(
            part.at[h, to_y * n_z + to_z], blocks.at[h, mine], rs_send.at[h], rs_recv.at[h],
            to_y * 2 + core, to_z * 2 + x,
        ).start()

    for k in range(1, len(rounds) - 1):
        close_round(k)
        open_round(k + 1)
    totals = [term(h, 0, flip_ref[...], me_g, me_d) for h in range(2)]
    close_round(len(rounds) - 1)
    open_round(len(rounds))
    flip_copies[0].wait_recv()
    for h in range(2):
        pair[h].wait_recv()
        totals[h] = totals[h] + term(h, 1, flips[0], pair_g, me_d)
    flip_copies[1].wait_recv()
    flip_copies[2].start()
    forward = []
    for h in range(2):
        for c in range(pieces // 2):
            at = pl.ds(c * piece, piece)
            k = h * (pieces // 2) + c
            twin[k].wait_recv()
            copy = remote(
                slabs.at[h, 2, at], slabs.at[h, 3, at],
                fwd_send.at[k], fwd_recv.at[k], pair_g, me_d,
            )
            copy.start()
            forward.append(copy)
        total = totals[h] + term(h, 2, flips[1], me_g, twin_d)
        if h == 0:
            flip_copies[2].wait_recv()
        for copy in forward[h * (pieces // 2):]:
            copy.wait_recv()
        total = total + term(h, 3, flips[2], pair_g, twin_d)
        total = total.reshape(groups, own, width)
        part[h] = jnp.where(
            left.reshape(1, 1, width), total[:, :own // 2], swap(total[:, own // 2:])
        )
        if h == 0:
            close_round(len(rounds))
            open_round(len(rounds) + 1)
        for i in range(n_y - 1, -1, -1):
            loop(n_z - (i == 0), lambda j: give(h, i, j + (i == 0)))
        blocks[h, mine] = part[h, mine]
    sums = []
    for h in range(2):
        others = blocks.at[h, pl.ds(0, groups - 1)]
        pltpu.make_async_copy(others, others, rs_recv.at[h]).wait()
        summed = blocks[h, 0]
        for i in range(1, groups):
            summed = summed + blocks[h, i]
        sums.append(summed)
    sketch = jnp.concatenate(
        [
            jnp.where(left, sums[0], swap(sums[1])),
            jnp.where(left, swap(sums[0]), sums[1]),
        ],
        axis=0,
    )
    sketch = sketch * (1.0 / math.sqrt(rows * devices))
    sketch_ref[...] = sketch

    close_round(len(rounds) + 1)
    chunks = gfull.shape[0]
    across = min(chunks, n_dev // 2)
    first = (n_dev - across) // 2
    chunk = width // chunks
    linear = me_g * n_dev + me_d
    reducer = (me_g < chunks // across) & (me_d >= first) & (me_d < first + across)
    my_chunk = me_g * across + me_d - first
    gram = lax.dot_general(
        sketch, sketch, (((0,), (0,)), ((), ())),
        precision=lax.Precision.HIGHEST, preferred_element_type=f32,
    )
    gpart[...] = gram.reshape(chunks, chunk, width)
    turn = lax.rem(linear, chunks)
    for k in range(chunks):
        to = lax.rem(k + turn, chunks)
        to_g, to_d = lax.div(to, across), first + lax.rem(to, across)

        @pl.when((me_g != to_g) | (me_d != to_d))
        def _():
            remote(gpart.at[to], gslots.at[linear], g_send, g_recv, to_g, to_d).start()

    @pl.when(reducer)
    def _():
        gslots[linear] = gpart[my_chunk]
        rest = gslots.at[pl.ds(0, devices - 1)]
        pltpu.make_async_copy(rest, rest, g_recv).wait()
        result = jnp.sum(gslots[...], axis=0) * (1.0 / samples)
        reduced[...] = result
        gfull[my_chunk] = result

        def tell(i, j):
            remote(
                reduced, gfull.at[my_chunk], b_send, b_recv,
                lax.rem(me_g + i, n_grp), lax.rem(me_d + j, n_dev),
            ).start()

        for i in range(n_grp - 1, -1, -1):
            loop(n_dev - (i == 0), lambda j: tell(i, j + (i == 0)))
        most = gfull.at[pl.ds(0, chunks - 1)]
        pltpu.make_async_copy(most, most, b_recv).wait()
        pltpu.make_async_copy(rest, rest, b_send).wait()
        pltpu.make_async_copy(most, most, g_send).wait()

    @pl.when(jnp.logical_not(reducer))
    def _():
        pltpu.make_async_copy(gfull, gfull, b_recv).wait()
        pltpu.make_async_copy(gfull, gfull, g_send).wait()

    gram_ref[...] = gfull[...].reshape(width, width)
    for copy in twin + forward + flip_copies + pair:
        copy.wait_send()
    for h in range(2):
        others = blocks.at[h, pl.ds(0, groups - 1)]
        pltpu.make_async_copy(others, others, rs_send.at[h]).wait()


def body(matrix, flip_bits, sample_rows):
    rows, width = matrix.shape
    n_grp, n_dev = lax.axis_size("grp"), lax.axis_size("dev")
    devices = n_grp * n_dev
    samples = sample_rows.shape[0]
    own = samples // devices
    groups = devices // 4
    chunks = min(width // 8, devices // 2)
    chunk = width // chunks
    pieces = 4
    f32, i32 = jnp.float32, jnp.int32
    dma = pltpu.SemaphoreType.DMA
    vmem = pl.BlockSpec(memory_space=pltpu.VMEM)
    return pl.pallas_call(
        functools.partial(kernel, n_grp, n_dev, rows, own),
        out_shape=(
            pltpu.VMEM((own, width), f32),
            pltpu.VMEM((width, width), f32),
        ),
        in_specs=[pl.BlockSpec(memory_space=pl.ANY)] * 3,
        out_specs=(vmem, vmem),
        scratch_shapes=[
            pltpu.VMEM((rows // LANES, LANES), i32),
            pltpu.VMEM((samples // LANES, LANES), i32),
            pltpu.VMEM((rows, width), f32),
            pltpu.VMEM((2, 4, rows // 2, width), f32),
            pltpu.VMEM((3, rows // LANES, LANES), i32),
            pltpu.VMEM((samples // 2, LANES), i32),
            pltpu.VMEM((groups * own, LANES), i32),
            pltpu.VMEM((groups * own, rows), jnp.bfloat16),
            pltpu.VMEM((2, groups, own // 2, width), f32),
            pltpu.VMEM((2, groups, own // 2, width), f32),
            pltpu.VMEM((chunks, chunk, width), f32),
            pltpu.VMEM((devices, chunk, width), f32),
            pltpu.VMEM((chunks, chunk, width), f32),
            pltpu.VMEM((chunk, width), f32),
            dma((3,)), dma((2,)), dma((2,)), dma((pieces,)), dma((pieces,)), dma((pieces,)), dma((pieces,)),
            dma((3,)), dma((3,)), dma((2,)), dma((2,)), dma, dma, dma, dma,
            pltpu.SemaphoreType.REGULAR((16,)),
        ],
        compiler_params=pltpu.CompilerParams(collective_id=0, has_side_effects=True),
    )(
        matrix,
        flip_bits.reshape(rows // LANES, LANES),
        sample_rows.reshape(samples // LANES, LANES),
    )


def solution(mesh):
    return jax.shard_map(
        body,
        mesh=mesh,
        in_specs=(P(("grp", "dev"), None), P(("grp", "dev")), P()),
        out_specs=(P(("grp", "dev"), None), P()),
        check_vma=False,
    )
```

profile of v0, /device:TPU:0, one launch (start us, length us, event | category | flops | bytes accessed | tf_op | source)
XLA Modules:
  0.0 33.0 jit_solution(4671183634231502082)
XLA Ops:
  0.6 31.1 %shard_map.50 = (f32[64,128]{1,0:T(8,128)S(1)}, f32[128,128]{1,0:T(8,128)S(1)}) custom-call(f32[512,128]{1,0:T(8,128)} %x_ref.1, s32[4,128]{1,0:T(4,128)} %bitcast.3, s32[16,128]{1,0:T(8,128)} %bitcast.2), custom_call_target="tpu_custom_call" | custom-call | tf_op jit(solution)/shard_map/pallas_call | solution.py:359
  31.8 0.6 %copy.7 = f32[64,128]{1,0:T(8,128)} copy(f32[64,128]{1,0:T(8,128)S(1)} %get-tuple-element.2) | data formatting | bytes 65536
  32.4 0.6 %copy.8 = f32[128,128]{1,0:T(8,128)} copy(f32[128,128]{1,0:T(8,128)S(1)} %get-tuple-element.3) | data formatting | bytes 131072
where the time goes:
time: 33.2 us; the launch traced here: 33 us
  Pallas kernels  31.1 us (94%)
  local copies, waits for them, and re-layouts  1.25 us (4%)
  between operations  0.64 us (2%)
    pallas_call x1, Pallas kernels, body(): pl.pallas_call(functools.partial(kernel, n_grp, n_dev, rows, own), out_sh...  31.1 us
    unnamed x2, local copies, waits for them, and re-layouts  1.25 us

commit v1 on v0

--- a/solution.py
+++ b/solution.py
@@ -343,7 +343,179 @@
         pltpu.make_async_copy(others, others, rs_send.at[h]).wait()
 
 
-def body(matrix, flip_bits, sample_rows):
+def split2(value):
+    high = value.astype(jnp.bfloat16)
+    return high, (value - high.astype(jnp.float32)).astype(jnp.bfloat16)
+
+
+def plane_kernel(
+    n_grp, n_dev, rows, own,
+    x_hbm, flip_hbm, sample_hbm, sketch_ref, gram_ref,
+    x_ref, flip_ref, sample_ref, turned, slabs, signs, peer_signs, part, blocks, mixed, cols, turn_back,
+    gpart, gslots, ghalf, gmine, gfull,
+    load_sem, in_send, in_recv, z_send, z_recv, out_send, out_recv, core_send, core_recv, gz_send, gz_recv,
+):
+    f32, bf16 = jnp.float32, jnp.bfloat16
+    width = x_ref.shape[1]
+    n_y, n_z = n_grp // 2, n_dev // 2
+    peers = n_grp * 2
+    mine = width // peers
+    span = n_dev * own // LANES
+    samples = sample_ref.shape[0] * LANES
+    picks = n_grp * LANES
+    row_bits = rows.bit_length() - 1
+    all_bits = (rows * n_grp * n_dev).bit_length() - 1
+    me_g, me_d = lax.axis_index("grp"), lax.axis_index("dev")
+    core, y = lax.rem(me_g, 2), lax.div(me_g, 2)
+    x, z = lax.rem(me_d, 2), lax.div(me_d, 2)
+    me = me_g * 2 + x
+
+    plane = [(a, k, b) for a in range(n_y) for k in range(2) for b in range(2)][:0:-1]
+    plane = sorted(plane, key=lambda at: -((at[0] > 0) + at[1]))
+
+    def peer(a, k, b):
+        to_y, to_x, to_c = lax.rem(y + a, n_y), lax.rem(x + k, 2), lax.rem(core + b, 2)
+        return to_y * 2 + to_c, to_x, to_c
+
+    def remote(src, dst, send, recv, grp, dev):
+        return pltpu.make_async_remote_copy(
+            src_ref=src, dst_ref=dst, send_sem=send, recv_sem=recv,
+            device_id=(grp, dev), device_id_type=MESH,
+        )
+
+    barrier = pltpu.get_barrier_semaphore()
+    loads = [
+        pltpu.make_async_copy(x_hbm, x_ref, load_sem.at[0]),
+        pltpu.make_async_copy(flip_hbm, flip_ref, load_sem.at[1]),
+        pltpu.make_async_copy(sample_hbm, sample_ref, load_sem.at[2]),
+    ]
+    for at in plane:
+        grp, to_x, _ = peer(*at)
+        pl.semaphore_signal(barrier, inc=1, device_id=(grp, z * 2 + to_x), device_id_type=MESH)
+    for d in range(1, n_z):
+        pl.semaphore_signal(
+            barrier, inc=1, device_id=(me_g, lax.rem(z + d, n_z) * 2 + x), device_id_type=MESH
+        )
+    for copy in loads:
+        copy.start()
+    for copy in loads:
+        copy.wait()
+
+    toggles = (1 - 2 * flip_ref[...]).astype(f32)
+    for k in range(rows // LANES):
+        at = slice(k * LANES, (k + 1) * LANES)
+        turned[:, at] = jnp.transpose(x_ref[at, :]) * toggles[k:k + 1, :]
+    pl.semaphore_wait(barrier, peers - 1 + n_z - 1)
+
+    sent = []
+    for m, at in enumerate(plane):
+        grp, to_x, _ = peer(*at)
+        to = grp * 2 + to_x
+        copy = remote(
+            turned.at[pl.ds(pl.multiple_of(to * mine, mine), mine)], slabs.at[me],
+            in_send.at[m], in_recv.at[m], grp, z * 2 + to_x,
+        )
+        copy.start()
+        sent.append(copy)
+    slabs[me] = turned[pl.ds(pl.multiple_of(me * mine, mine), mine), :]
+
+    order = sorted(range(n_z), key=lambda d: -min(d, n_z - d))
+    low = lax.broadcasted_iota(jnp.int32, (16, LANES), 0)
+    for i, d in enumerate(order):
+        to_z = lax.rem(z + d, n_z)
+        for g in range(n_grp):
+            wanted = sample_ref[pl.ds(g * span + to_z, 1), :]
+            wide = jnp.broadcast_to(wanted, (16, LANES))
+            pieces = [sign_of(wide & low, 16).astype(bf16)]
+            for bit in range(4, row_bits):
+                factor = (1 - 2 * ((wide >> bit) & 1)).astype(f32).astype(bf16)
+                pieces += [piece * factor for piece in pieces]
+            for k, piece in enumerate(pieces):
+                signs[i, k * 16:(k + 1) * 16, g * LANES:(g + 1) * LANES] = piece
+            wide = wide[:8]
+            for p in range(peers):
+                holder = ((p // 2) * n_dev + z * 2 + p % 2) * rows
+                peer_signs[i, p, :, g * LANES:(g + 1) * LANES] = sign_of(wide & holder, all_bits)
+
+    for copy in sent:
+        copy.wait_recv()
+    high, mid = split2(slabs[...].reshape(peers * mine, rows))
+    left = jnp.concatenate([high, mid], axis=0)
+    passed = []
+    for i, d in enumerate(order):
+        product = jnp.dot(left, signs[i], preferred_element_type=f32)
+        product = product[:peers * mine] + product[peers * mine:]
+        total = None
+        for p in range(peers):
+            term = product[p * mine:(p + 1) * mine].reshape(mine // 8, 8, picks) * peer_signs[i, p][None]
+            total = term if total is None else total + term
+        part[i] = total.reshape(mine, picks)
+        if d:
+            copy = remote(
+                part.at[i], blocks.at[i], z_send.at[i], z_recv.at[i],
+                me_g, lax.rem(z + d, n_z) * 2 + x,
+            )
+            copy.start()
+            passed.append(copy)
+    total = part[n_z - 1]
+    for i, copy in enumerate(passed):
+        copy.wait_recv()
+        total = total + blocks[i]
+    total = total * (1.0 / math.sqrt(rows * n_grp * n_dev))
+    for c in range(2):
+        mixed[c] = jnp.concatenate(
+            [total[:, g * LANES:(g + 1) * LANES] for g in range(c, n_grp, 2)], axis=1
+        )
+    given = []
+    for m, at in enumerate(plane):
+        grp, to_x, to_c = peer(*at)
+        copy = remote(
+            mixed.at[to_c], cols.at[me], out_send.at[m], out_recv.at[m], grp, z * 2 + to_x
+        )
+        copy.start()
+        given.append(copy)
+    cols[me] = mixed[core]
+    for copy in given:
+        copy.wait_recv()
+
+    held = cols[...].reshape(width, n_y * LANES)
+    high, mid = split2(held)
+    gram = lax.dot_general(
+        jnp.concatenate([high, mid, high], axis=1), jnp.concatenate([high, high, mid], axis=1),
+        (((1,), (1,)), ((), ())), preferred_element_type=f32,
+    )
+    half = width // 2
+    gpart[...] = (gram * (1.0 / samples)).reshape(2, half, width)
+    sibling = me_g + 1 - 2 * core
+    swap = remote(gpart.at[1 - core], gslots, core_send.at[0], core_recv.at[0], sibling, me_d)
+    swap.start()
+    block = cols[:, :, pl.ds(pl.multiple_of(y * LANES, LANES), LANES)].reshape(width, LANES)
+    turn_back[...] = jnp.transpose(block)
+    sketch_ref[...] = turn_back[pl.ds(pl.multiple_of(x * own, own), own), :]
+    swap.wait_recv()
+    gmine[...] = gpart[core] + gslots[...]
+    around = []
+    for d in range(1, n_z):
+        copy = remote(
+            gmine, ghalf.at[d - 1], gz_send.at[d - 1], gz_recv.at[d - 1],
+            me_g, lax.rem(z + d, n_z) * 2 + x,
+        )
+        copy.start()
+        around.append(copy)
+    result = gmine[...]
+    for i, copy in enumerate(around):
+        copy.wait_recv()
+        result = result + ghalf[i]
+    gfull[core] = result
+    last = remote(gfull.at[core], gfull.at[core], core_send.at[1], core_recv.at[1], sibling, me_d)
+    last.start()
+    last.wait_recv()
+    gram_ref[...] = gfull[...].reshape(width, width)
+    for copy in sent + passed + given + around + [swap, last]:
+        copy.wait_send()
+
+
+def general(matrix, flip_bits, sample_rows):
     rows, width = matrix.shape
     n_grp, n_dev = lax.axis_size("grp"), lax.axis_size("dev")
     devices = n_grp * n_dev
@@ -391,6 +563,60 @@
     )
 
 
+def plane_body(matrix, flip_bits, sample_rows):
+    rows, width = matrix.shape
+    n_grp, n_dev = lax.axis_size("grp"), lax.axis_size("dev")
+    samples = sample_rows.shape[0]
+    own = samples // (n_grp * n_dev)
+    n_y, n_z, peers = n_grp // 2, n_dev // 2, n_grp * 2
+    mine, picks, half = width // peers, n_grp * LANES, width // 2
+    f32, i32, bf16 = jnp.float32, jnp.int32, jnp.bfloat16
+    dma = pltpu.SemaphoreType.DMA
+    vmem = pl.BlockSpec(memory_space=pltpu.VMEM)
+    return pl.pallas_call(
+        functools.partial(plane_kernel, n_grp, n_dev, rows, own),
+        out_shape=(pltpu.VMEM((own, width), f32), pltpu.VMEM((width, width), f32)),
+        in_specs=[pl.BlockSpec(memory_space=pl.ANY)] * 3,
+        out_specs=(vmem, vmem),
+        scratch_shapes=[
+            pltpu.VMEM((rows, width), f32),
+            pltpu.VMEM((rows // LANES, LANES), i32),
+            pltpu.VMEM((samples // LANES, LANES), i32),
+            pltpu.VMEM((width, rows), f32),
+            pltpu.VMEM((peers, mine, rows), f32),
+            pltpu.VMEM((n_z, rows, picks), bf16),
+            pltpu.VMEM((n_z, peers, 8, picks), f32),
+            pltpu.VMEM((n_z, mine, picks), f32),
+            pltpu.VMEM((n_z - 1, mine, picks), f32),
+            pltpu.VMEM((2, mine, n_y * LANES), f32),
+            pltpu.VMEM((peers, mine, n_y * LANES), f32),
+            pltpu.VMEM((LANES, width), f32),
+            pltpu.VMEM((2, half, width), f32),
+            pltpu.VMEM((half, width), f32),
+            pltpu.VMEM((n_z - 1, half, width), f32),
+            pltpu.VMEM((half, width), f32),
+            pltpu.VMEM((2, half, width), f32),
+            dma((3,)), dma((peers - 1,)), dma((peers - 1,)), dma((n_z - 1,)), dma((n_z - 1,)),
+            dma((peers - 1,)), dma((peers - 1,)), dma((2,)), dma((2,)), dma((n_z - 1,)), dma((n_z - 1,)),
+        ],
+        compiler_params=pltpu.CompilerParams(collective_id=0, has_side_effects=True),
+    )(
+        matrix,
+        flip_bits.reshape(rows // LANES, LANES),
+        sample_rows.reshape(samples // LANES, LANES),
+    )
+
+
+def body(matrix, flip_bits, sample_rows):
+    rows, width = matrix.shape
+    n_grp, n_dev = lax.axis_size("grp"), lax.axis_size("dev")
+    paired = sample_rows.shape[0] * 2 == n_grp * n_dev * LANES
+    tiled = width == LANES and width % (n_grp * 2 * 8) == 0
+    if paired and tiled and rows % LANES == 0:
+        return plane_body(matrix, flip_bits, sample_rows)
+    return general(matrix, flip_bits, sample_rows)
+
+
 def solution(mesh):
     return jax.shard_map(
         body,

time: 33.2 us -> 27 us (0.81)
  Pallas kernels: 31.1 us -> 25 us
    pallas_call x1, Pallas kernels: 31.1 us -> 25 us  [plane_body(): pl.pallas_call(functools.partial(plane_kernel, n_grp, n_dev, rows, own),...]
where the time goes in v1:
time: 27 us; the launch traced here: 26.9 us
  Pallas kernels  25 us (93%)
  local copies, waits for them, and re-layouts  1.25 us (5%)
  between operations  0.64 us (2%)
    pallas_call x1, Pallas kernels, plane_body(): pl.pallas_call(functools.partial(plane_kernel, n_grp, n_dev, rows, own),...  25 us
    unnamed x2, local copies, waits for them, and re-layouts  1.25 us

profile of v1, /device:TPU:0, one launch (start us, length us, event | category | flops | bytes accessed | tf_op | source)
XLA Modules:
  0.0 26.9 jit_solution(2705571865378411082)
XLA Ops:
  0.6 25.0 %shard_map.50 = (f32[64,128]{1,0:T(8,128)S(1)}, f32[128,128]{1,0:T(8,128)S(1)}) custom-call(f32[512,128]{1,0:T(8,128)} %x_hbm.1, s32[4,128]{1,0:T(4,128)} %bitcast.3, s32[16,128]{1,0:T(8,128)} %bitcast.2), custom_call_target="tpu_custom_call" | custom-call | tf_op jit(solution)/shard_map/pallas_call | solution.py:576
  25.6 0.6 %copy.7 = f32[64,128]{1,0:T(8,128)} copy(f32[64,128]{1,0:T(8,128)S(1)} %get-tuple-element.2) | data formatting | bytes 65536
  26.2 0.6 %copy.8 = f32[128,128]{1,0:T(8,128)} copy(f32[128,128]{1,0:T(8,128)S(1)} %get-tuple-element.3) | data formatting | bytes 131072

commit v2 on v0

--- a/solution.py
+++ b/solution.py
@@ -343,7 +343,180 @@
         pltpu.make_async_copy(others, others, rs_send.at[h]).wait()
 
 
-def body(matrix, flip_bits, sample_rows):
+def split2(value):
+    high = value.astype(jnp.bfloat16)
+    return high, (value - high.astype(jnp.float32)).astype(jnp.bfloat16)
+
+
+def plane_kernel(
+    n_grp, n_dev, rows, own,
+    x_hbm, flip_hbm, sample_hbm, sketch_ref, gram_ref,
+    x_ref, flip_ref, sample_ref, turned, slabs, signs, peer_signs, part, blocks, mixed, cols, turn_back,
+    gram_out, gram_in,
+    load_sem, in_send, in_recv, z_send, z_recv, out_send, out_recv, g_send, g_recv,
+):
+    f32, bf16 = jnp.float32, jnp.bfloat16
+    width = x_ref.shape[1]
+    n_y, n_z = n_grp // 2, n_dev // 2
+    peers = n_grp * 2
+    half = width // 2
+    mine = half // peers
+    span = n_dev * own // LANES
+    samples = sample_ref.shape[0] * LANES
+    picks = n_grp * LANES
+    row_bits = rows.bit_length() - 1
+    all_bits = (rows * n_grp * n_dev).bit_length() - 1
+    me_g, me_d = lax.axis_index("grp"), lax.axis_index("dev")
+    core, y = lax.rem(me_g, 2), lax.div(me_g, 2)
+    x, z = lax.rem(me_d, 2), lax.div(me_d, 2)
+    me = me_g * 2 + x
+
+    plane = [(a, k, b) for a in range(n_y) for k in range(2) for b in range(2)][:0:-1]
+    plane = sorted(plane, key=lambda at: -((at[0] > 0) + at[1]))
+    order = sorted(range(n_z), key=lambda d: -min(d, n_z - d))
+    ring = [(d, b) for d in order for b in range(2) if d or b]
+
+    def peer(a, k, b):
+        to_y, to_x, to_c = lax.rem(y + a, n_y), lax.rem(x + k, 2), lax.rem(core + b, 2)
+        return to_y * 2 + to_c, z * 2 + to_x
+
+    def along(d, b):
+        return y * 2 + lax.rem(core + b, 2), lax.rem(z + d, n_z) * 2 + x
+
+    def remote(src, dst, send, recv, at):
+        return pltpu.make_async_remote_copy(
+            src_ref=src, dst_ref=dst, send_sem=send, recv_sem=recv,
+            device_id=at, device_id_type=MESH,
+        )
+
+    barrier = pltpu.get_barrier_semaphore()
+    loads = [
+        pltpu.make_async_copy(x_hbm, x_ref, load_sem.at[0]),
+        pltpu.make_async_copy(flip_hbm, flip_ref, load_sem.at[1]),
+        pltpu.make_async_copy(sample_hbm, sample_ref, load_sem.at[2]),
+    ]
+    for copy in loads:
+        copy.start()
+    greeted = [peer(*at) for at in plane] + [along(*at) for at in ring if at[0]]
+    for at in greeted:
+        pl.semaphore_signal(barrier, inc=1, device_id=at, device_id_type=MESH)
+    for copy in loads:
+        copy.wait()
+
+    toggles = (1 - 2 * flip_ref[...]).astype(f32)
+    for k in range(rows // LANES):
+        at = slice(k * LANES, (k + 1) * LANES)
+        turned[:, at] = jnp.transpose(x_ref[at, :]) * toggles[k:k + 1, :]
+    pl.semaphore_wait(barrier, len(greeted))
+
+    sent = []
+    for h in range(2):
+        for m, at in enumerate(plane):
+            grp, dev = peer(*at)
+            to = grp * 2 + lax.rem(dev, 2)
+            copy = remote(
+                turned.at[pl.ds(pl.multiple_of(h * half + to * mine, mine), mine)],
+                slabs.at[h, me], in_send.at[h, m], in_recv.at[h, m], (grp, dev),
+            )
+            copy.start()
+            sent.append(copy)
+        slabs[h, me] = turned[pl.ds(pl.multiple_of(h * half + me * mine, mine), mine), :]
+
+    low = lax.broadcasted_iota(jnp.int32, (16, LANES), 0)
+    for i, d in enumerate(order):
+        to_z = lax.rem(z + d, n_z)
+        for g in range(n_grp):
+            wanted = sample_ref[pl.ds(g * span + to_z, 1), :]
+            wide = jnp.broadcast_to(wanted, (16, LANES))
+            pieces = [sign_of(wide & low, 16).astype(bf16)]
+            for bit in range(4, row_bits):
+                factor = (1 - 2 * ((wide >> bit) & 1)).astype(f32).astype(bf16)
+                pieces += [piece * factor for piece in pieces]
+            for k, piece in enumerate(pieces):
+                signs[i, k * 16:(k + 1) * 16, g * LANES:(g + 1) * LANES] = piece
+            wide = wide[:8]
+            for p in range(peers):
+                holder = ((p // 2) * n_dev + z * 2 + p % 2) * rows
+                peer_signs[i, p, :, g * LANES:(g + 1) * LANES] = sign_of(wide & holder, all_bits)
+
+    passed = []
+    for h in range(2):
+        for copy in sent[h * len(plane):(h + 1) * len(plane)]:
+            copy.wait_recv()
+        high, mid = split2(slabs[h].reshape(half, rows))
+        left = jnp.concatenate([high, mid], axis=0)
+        for i, d in enumerate(order):
+            product = jnp.dot(left, signs[i], preferred_element_type=f32)
+            product = product[:half] + product[half:]
+            total = None
+            for p in range(peers):
+                term = product[p * mine:(p + 1) * mine].reshape(mine // 8, 8, picks) * peer_signs[i, p][None]
+                total = term if total is None else total + term
+            part[h, i] = total.reshape(mine, picks)
+            if d:
+                copy = remote(
+                    part.at[h, i], blocks.at[h, i], z_send.at[h, i], z_recv.at[h, i], along(d, 0)
+                )
+                copy.start()
+                passed.append(copy)
+    given = []
+    for h in range(2):
+        total = part[h, n_z - 1]
+        for i, copy in enumerate(passed[h * (n_z - 1):(h + 1) * (n_z - 1)]):
+            copy.wait_recv()
+            total = total + blocks[h, i]
+        mixed[h] = total * (1.0 / math.sqrt(rows * n_grp * n_dev))
+        for m, at in enumerate(plane):
+            copy = remote(
+                mixed.at[h], cols.at[h, me], out_send.at[h, m], out_recv.at[h, m], peer(*at)
+            )
+            copy.start()
+            given.append(copy)
+        cols[h, me] = mixed[h]
+
+    around = []
+    right = None
+    for h in range(2):
+        for copy in given[h * len(plane):(h + 1) * len(plane)]:
+            copy.wait_recv()
+        high, mid = split2(cols[h].reshape(half, picks))
+        fresh = jnp.concatenate([high, high, mid], axis=1)
+        right = fresh if right is None else jnp.concatenate([right, fresh], axis=0)
+        high, mid = split2(cols[h, pl.ds(core * (peers // 2), peers // 2)].reshape(half // 2, picks))
+        gram = lax.dot_general(
+            jnp.concatenate([high, mid, high], axis=1), right,
+            (((1,), (1,)), ((), ())), preferred_element_type=f32,
+        )
+        if h == 0:
+            gram = jnp.concatenate([gram, jnp.zeros_like(gram)], axis=1)
+        gram_out[h] = gram * (1.0 / samples)
+        for m, (d, b) in enumerate(ring):
+            copy = remote(
+                gram_out.at[h], gram_in.at[h, d, core], g_send.at[h, m], g_recv.at[h, m], along(d, b)
+            )
+            copy.start()
+            around.append(copy)
+        gram_in[h, 0, core] = gram_out[h]
+
+    block = cols[:, :, :, pl.ds(pl.multiple_of(me_g * LANES, LANES), LANES)].reshape(width, LANES)
+    turn_back[...] = jnp.transpose(block)
+    sketch_ref[...] = turn_back[pl.ds(pl.multiple_of(x * own, own), own), :]
+    result = []
+    for h in range(2):
+        for copy in around[h * len(ring):(h + 1) * len(ring)]:
+            copy.wait_recv()
+        total = gram_in[h, 0]
+        for d in range(1, n_z):
+            total = total + gram_in[h, d]
+        result.append(total.reshape(half, width))
+    cross = jnp.transpose(result[1])[:half]
+    gram_ref[:half, :] = jnp.concatenate([result[0][:, :half], cross], axis=1)
+    gram_ref[half:, :] = result[1]
+    for copy in sent + passed + given + around:
+        copy.wait_send()
+
+
+def general(matrix, flip_bits, sample_rows):
     rows, width = matrix.shape
     n_grp, n_dev = lax.axis_size("grp"), lax.axis_size("dev")
     devices = n_grp * n_dev
@@ -391,6 +564,57 @@
     )
 
 
+def plane_body(matrix, flip_bits, sample_rows):
+    rows, width = matrix.shape
+    n_grp, n_dev = lax.axis_size("grp"), lax.axis_size("dev")
+    samples = sample_rows.shape[0]
+    own = samples // (n_grp * n_dev)
+    n_z, peers = n_dev // 2, n_grp * 2
+    mine, picks, half = width // peers // 2, n_grp * LANES, width // 2
+    f32, i32, bf16 = jnp.float32, jnp.int32, jnp.bfloat16
+    dma = pltpu.SemaphoreType.DMA
+    vmem = pl.BlockSpec(memory_space=pltpu.VMEM)
+    return pl.pallas_call(
+        functools.partial(plane_kernel, n_grp, n_dev, rows, own),
+        out_shape=(pltpu.VMEM((own, width), f32), pltpu.VMEM((width, width), f32)),
+        in_specs=[pl.BlockSpec(memory_space=pl.ANY)] * 3,
+        out_specs=(vmem, vmem),
+        scratch_shapes=[
+            pltpu.VMEM((rows, width), f32),
+            pltpu.VMEM((rows // LANES, LANES), i32),
+            pltpu.VMEM((samples // LANES, LANES), i32),
+            pltpu.VMEM((width, rows), f32),
+            pltpu.VMEM((2, peers, mine, rows), f32),
+            pltpu.VMEM((n_z, rows, picks), bf16),
+            pltpu.VMEM((n_z, peers, 8, picks), f32),
+            pltpu.VMEM((2, n_z, mine, picks), f32),
+            pltpu.VMEM((2, n_z - 1, mine, picks), f32),
+            pltpu.VMEM((2, mine, picks), f32),
+            pltpu.VMEM((2, peers, mine, picks), f32),
+            pltpu.VMEM((LANES, width), f32),
+            pltpu.VMEM((2, half // 2, width), f32),
+            pltpu.VMEM((2, n_z, 2, half // 2, width), f32),
+            dma((3,)), dma((2, peers - 1)), dma((2, peers - 1)), dma((2, n_z - 1)), dma((2, n_z - 1)),
+            dma((2, peers - 1)), dma((2, peers - 1)), dma((2, 2 * n_z - 1)), dma((2, 2 * n_z - 1)),
+        ],
+        compiler_params=pltpu.CompilerParams(collective_id=0, has_side_effects=True),
+    )(
+        matrix,
+        flip_bits.reshape(rows // LANES, LANES),
+        sample_rows.reshape(samples // LANES, LANES),
+    )
+
+
+def body(matrix, flip_bits, sample_rows):
+    rows, width = matrix.shape
+    n_grp, n_dev = lax.axis_size("grp"), lax.axis_size("dev")
+    paired = sample_rows.shape[0] * 2 == n_grp * n_dev * LANES
+    tiled = width == LANES and width % (n_grp * 2 * 16) == 0
+    if paired and tiled and rows % LANES == 0:
+        return plane_body(matrix, flip_bits, sample_rows)
+    return general(matrix, flip_bits, sample_rows)
+
+
 def solution(mesh):
     return jax.shard_map(
         body,

time: 33.2 us -> 28 us (0.84)
  Pallas kernels: 31.1 us -> 26 us
    pallas_call x1, Pallas kernels: 31.1 us -> 26 us  [plane_body(): pl.pallas_call(functools.partial(plane_kernel, n_grp, n_dev, rows, own),...]
where the time goes in v2:
time: 28 us; the launch traced here: 27.9 us
  Pallas kernels  26 us (93%)
  local copies, waits for them, and re-layouts  1.25 us (4%)
  between operations  0.64 us (2%)
    pallas_call x1, Pallas kernels, plane_body(): pl.pallas_call(functools.partial(plane_kernel, n_grp, n_dev, rows, own),...  26 us
    unnamed x2, local copies, waits for them, and re-layouts  1.25 us

profile of v2, /device:TPU:0, one launch (start us, length us, event | category | flops | bytes accessed | tf_op | source)
XLA Modules:
  0.0 27.9 jit_solution(18224087199188837514)
XLA Ops:
  0.6 26.0 %shard_map.50 = (f32[64,128]{1,0:T(8,128)S(1)}, f32[128,128]{1,0:T(8,128)S(1)}) custom-call(f32[512,128]{1,0:T(8,128)} %x_hbm.1, s32[4,128]{1,0:T(4,128)} %bitcast.3, s32[16,128]{1,0:T(8,128)} %bitcast.2), custom_call_target="tpu_custom_call" | custom-call | tf_op jit(solution)/shard_map/pallas_call | solution.py:577
  26.6 0.6 %copy.7 = f32[64,128]{1,0:T(8,128)} copy(f32[64,128]{1,0:T(8,128)S(1)} %get-tuple-element.2) | data formatting | bytes 65536
  27.2 0.6 %copy.8 = f32[128,128]{1,0:T(8,128)} copy(f32[128,128]{1,0:T(8,128)S(1)} %get-tuple-element.3) | data formatting | bytes 131072

commit v3 on v2

--- a/solution.py
+++ b/solution.py
@@ -351,43 +351,44 @@
 def plane_kernel(
     n_grp, n_dev, rows, own,
     x_hbm, flip_hbm, sample_hbm, sketch_ref, gram_ref,
-    x_ref, flip_ref, sample_ref, turned, slabs, signs, peer_signs, part, blocks, mixed, cols, turn_back,
-    gram_out, gram_in,
-    load_sem, in_send, in_recv, z_send, z_recv, out_send, out_recv, g_send, g_recv,
+    x_ref, flip_ref, sample_ref, turned, slabs, signs, peer_signs, lent, borrowed, part, blocks, mixed, cols,
+    turn_back, gram_out, gram_in, gram_sum, gram_far, lower,
+    load_sem, in_send, in_recv, c_send, c_recv, z_send, z_recv, out_send, out_recv,
+    g_send, g_recv, h_send, h_recv,
 ):
     f32, bf16 = jnp.float32, jnp.bfloat16
     width = x_ref.shape[1]
     n_y, n_z = n_grp // 2, n_dev // 2
-    peers = n_grp * 2
-    half = width // 2
-    mine = half // peers
+    chips = n_y * 2
+    chunks, mine = slabs.shape[0], slabs.shape[2]
+    band = chips * mine
     span = n_dev * own // LANES
     samples = sample_ref.shape[0] * LANES
-    picks = n_grp * LANES
+    picks = n_y * LANES
     row_bits = rows.bit_length() - 1
     all_bits = (rows * n_grp * n_dev).bit_length() - 1
     me_g, me_d = lax.axis_index("grp"), lax.axis_index("dev")
     core, y = lax.rem(me_g, 2), lax.div(me_g, 2)
     x, z = lax.rem(me_d, 2), lax.div(me_d, 2)
-    me = me_g * 2 + x
-
-    plane = [(a, k, b) for a in range(n_y) for k in range(2) for b in range(2)][:0:-1]
-    plane = sorted(plane, key=lambda at: -((at[0] > 0) + at[1]))
+    me = y * 2 + x
+
+    plane = [(a, k) for a in range(n_y - 1, -1, -1) for k in (1, 0) if a or k]
     order = sorted(range(n_z), key=lambda d: -min(d, n_z - d))
-    ring = [(d, b) for d in order for b in range(2) if d or b]
-
-    def peer(a, k, b):
-        to_y, to_x, to_c = lax.rem(y + a, n_y), lax.rem(x + k, 2), lax.rem(core + b, 2)
-        return to_y * 2 + to_c, z * 2 + to_x
-
-    def along(d, b):
-        return y * 2 + lax.rem(core + b, 2), lax.rem(z + d, n_z) * 2 + x
+    sibling = (me_g + 1 - 2 * core, me_d)
+
+    def across(a, k):
+        to_y, to_x = lax.rem(y + a, n_y), lax.rem(x + k, 2)
+        return (to_y * 2 + core, z * 2 + to_x), to_y * 2 + to_x
+
+    def along(d):
+        return me_g, lax.rem(z + d, n_z) * 2 + x
 
     def remote(src, dst, send, recv, at):
         return pltpu.make_async_remote_copy(
             src_ref=src, dst_ref=dst, send_sem=send, recv_sem=recv,
             device_id=at, device_id_type=MESH,
         )
+
 
     barrier = pltpu.get_barrier_semaphore()
     loads = [
@@ -397,7 +398,7 @@
     ]
     for copy in loads:
         copy.start()
-    greeted = [peer(*at) for at in plane] + [along(*at) for at in ring if at[0]]
+    greeted = [across(*at)[0] for at in plane] + [along(d) for d in order[:-1]] + [sibling]
     for at in greeted:
         pl.semaphore_signal(barrier, inc=1, device_id=at, device_id_type=MESH)
     for copy in loads:
@@ -409,110 +410,142 @@
         turned[:, at] = jnp.transpose(x_ref[at, :]) * toggles[k:k + 1, :]
     pl.semaphore_wait(barrier, len(greeted))
 
-    sent = []
-    for h in range(2):
+    sent, swaps, passed, given, around, last = [], [], [], [], [], []
+    for k in range(chunks):
         for m, at in enumerate(plane):
-            grp, dev = peer(*at)
-            to = grp * 2 + lax.rem(dev, 2)
+            to, chip = across(*at)
             copy = remote(
-                turned.at[pl.ds(pl.multiple_of(h * half + to * mine, mine), mine)],
-                slabs.at[h, me], in_send.at[h, m], in_recv.at[h, m], (grp, dev),
+                turned.at[pl.ds(pl.multiple_of(k * band + chip * mine, mine), mine)],
+                slabs.at[k, me], in_send.at[k, m], in_recv.at[k, m], to,
             )
             copy.start()
             sent.append(copy)
-        slabs[h, me] = turned[pl.ds(pl.multiple_of(h * half + me * mine, mine), mine), :]
+    for k in range(chunks):
+        slabs[k, me] = turned[pl.ds(pl.multiple_of(k * band + me * mine, mine), mine), :]
 
     low = lax.broadcasted_iota(jnp.int32, (16, LANES), 0)
-    for i, d in enumerate(order):
-        to_z = lax.rem(z + d, n_z)
-        for g in range(n_grp):
-            wanted = sample_ref[pl.ds(g * span + to_z, 1), :]
-            wide = jnp.broadcast_to(wanted, (16, LANES))
-            pieces = [sign_of(wide & low, 16).astype(bf16)]
-            for bit in range(4, row_bits):
-                factor = (1 - 2 * ((wide >> bit) & 1)).astype(f32).astype(bf16)
-                pieces += [piece * factor for piece in pieces]
-            for k, piece in enumerate(pieces):
-                signs[i, k * 16:(k + 1) * 16, g * LANES:(g + 1) * LANES] = piece
-            wide = wide[:8]
-            for p in range(peers):
-                holder = ((p // 2) * n_dev + z * 2 + p % 2) * rows
-                peer_signs[i, p, :, g * LANES:(g + 1) * LANES] = sign_of(wide & holder, all_bits)
-
-    passed = []
-    for h in range(2):
-        for copy in sent[h * len(plane):(h + 1) * len(plane)]:
-            copy.wait_recv()
-        high, mid = split2(slabs[h].reshape(half, rows))
-        left = jnp.concatenate([high, mid], axis=0)
+    for r in range(2):
+        owner = core if r else 1 - core
         for i, d in enumerate(order):
-            product = jnp.dot(left, signs[i], preferred_element_type=f32)
-            product = product[:half] + product[half:]
-            total = None
-            for p in range(peers):
-                term = product[p * mine:(p + 1) * mine].reshape(mine // 8, 8, picks) * peer_signs[i, p][None]
-                total = term if total is None else total + term
-            part[h, i] = total.reshape(mine, picks)
+            to_z = lax.rem(z + d, n_z)
+            for j in range(n_y):
+                at = slice(i * picks + j * LANES, i * picks + (j + 1) * LANES)
+                wanted = sample_ref[pl.ds((j * 2 + owner) * span + to_z, 1), :]
+                wide = jnp.broadcast_to(wanted, (16, LANES))
+                pieces = [sign_of(wide & low, 16).astype(bf16)]
+                for bit in range(4, row_bits):
+                    factor = (1 - 2 * ((wide >> bit) & 1)).astype(f32).astype(bf16)
+                    pieces += [piece * factor for piece in pieces]
+                for k, piece in enumerate(pieces):
+                    signs[r, k * 16:(k + 1) * 16, at] = piece
+                wide = wide[:8]
+                for q in range(chips):
+                    holder = ((q // 2 * 2 + core) * n_dev + z * 2 + q % 2) * rows
+                    peer_signs[r, q, :, at] = sign_of(wide & holder, all_bits)
+
+    def halves(k):
+        high, mid = split2(slabs[k].reshape(band, rows))
+        return jnp.concatenate([high, mid], axis=0)
+
+    def partial(left, r):
+        product = jnp.dot(left, signs[r], preferred_element_type=f32)
+        product = product[:band] + product[band:]
+        total = None
+        for q in range(chips):
+            term = product[q * mine:(q + 1) * mine] * peer_signs[r, q]
+            total = term if total is None else total + term
+        return total
+
+    def settle(k):
+        swaps[k].wait_recv()
+        for i, d in enumerate(order):
+            at = slice(i * picks, (i + 1) * picks)
+            part[k, i] = part[k, i] + borrowed[k, :, at]
             if d:
                 copy = remote(
-                    part.at[h, i], blocks.at[h, i], z_send.at[h, i], z_recv.at[h, i], along(d, 0)
+                    part.at[k, i], blocks.at[k, i], z_send.at[k, i], z_recv.at[k, i], along(d)
                 )
                 copy.start()
                 passed.append(copy)
-    given = []
-    for h in range(2):
-        total = part[h, n_z - 1]
-        for i, copy in enumerate(passed[h * (n_z - 1):(h + 1) * (n_z - 1)]):
+
+    for k in range(chunks):
+        for copy in sent[k * len(plane):(k + 1) * len(plane)]:
             copy.wait_recv()
-            total = total + blocks[h, i]
-        mixed[h] = total * (1.0 / math.sqrt(rows * n_grp * n_dev))
+        left = halves(k)
+        lent[k] = partial(left, 0)
+        copy = remote(lent.at[k], borrowed.at[k], c_send.at[k], c_recv.at[k], sibling)
+        copy.start()
+        swaps.append(copy)
+        if k:
+            settle(k - 1)
+        mixture = partial(left, 1)
+        for i in range(n_z):
+            part[k, i] = mixture[:, i * picks:(i + 1) * picks]
+    settle(chunks - 1)
+    for k in range(chunks):
+        total = part[k, n_z - 1]
+        for i, copy in enumerate(passed[k * (n_z - 1):(k + 1) * (n_z - 1)]):
+            copy.wait_recv()
+            total = total + blocks[k, i]
+        mixed[k] = total * (1.0 / math.sqrt(rows * n_grp * n_dev))
         for m, at in enumerate(plane):
             copy = remote(
-                mixed.at[h], cols.at[h, me], out_send.at[h, m], out_recv.at[h, m], peer(*at)
+                mixed.at[k], cols.at[k, me], out_send.at[k, m], out_recv.at[k, m], across(*at)[0]
             )
             copy.start()
             given.append(copy)
-        cols[h, me] = mixed[h]
-
-    around = []
-    right = None
-    for h in range(2):
-        for copy in given[h * len(plane):(h + 1) * len(plane)]:
+        cols[k, me] = mixed[k]
+
+    right, held = None, None
+    for k in range(chunks):
+        for copy in given[k * len(plane):(k + 1) * len(plane)]:
             copy.wait_recv()
-        high, mid = split2(cols[h].reshape(half, picks))
+        high, mid = split2(cols[k].reshape(band, picks))
         fresh = jnp.concatenate([high, high, mid], axis=1)
         right = fresh if right is None else jnp.concatenate([right, fresh], axis=0)
-        high, mid = split2(cols[h, pl.ds(core * (peers // 2), peers // 2)].reshape(half // 2, picks))
         gram = lax.dot_general(
             jnp.concatenate([high, mid, high], axis=1), right,
             (((1,), (1,)), ((), ())), preferred_element_type=f32,
-        )
-        if h == 0:
-            gram = jnp.concatenate([gram, jnp.zeros_like(gram)], axis=1)
-        gram_out[h] = gram * (1.0 / samples)
-        for m, (d, b) in enumerate(ring):
+        ) * (1.0 / samples)
+        if k == 0:
+            held = gram
+            continue
+        if k == 1:
+            gram = jnp.concatenate([gram, held], axis=1)
+        room = width - gram.shape[1]
+        if room:
+            gram = jnp.concatenate([gram, jnp.zeros((band, room), f32)], axis=1)
+        gram_out[k - 1] = gram
+        for i, d in enumerate(order[:-1]):
             copy = remote(
-                gram_out.at[h], gram_in.at[h, d, core], g_send.at[h, m], g_recv.at[h, m], along(d, b)
+                gram_out.at[k - 1], gram_in.at[k - 1, i], g_send.at[k - 1, i], g_recv.at[k - 1, i], along(d)
             )
             copy.start()
             around.append(copy)
-        gram_in[h, 0, core] = gram_out[h]
-
-    block = cols[:, :, :, pl.ds(pl.multiple_of(me_g * LANES, LANES), LANES)].reshape(width, LANES)
+
+    block = cols[:, :, :, pl.ds(pl.multiple_of(y * LANES, LANES), LANES)].reshape(width, LANES)
     turn_back[...] = jnp.transpose(block)
     sketch_ref[...] = turn_back[pl.ds(pl.multiple_of(x * own, own), own), :]
-    result = []
-    for h in range(2):
-        for copy in around[h * len(ring):(h + 1) * len(ring)]:
+    for k in range(chunks - 1):
+        total = gram_out[k]
+        for i, copy in enumerate(around[k * (n_z - 1):(k + 1) * (n_z - 1)]):
             copy.wait_recv()
-        total = gram_in[h, 0]
-        for d in range(1, n_z):
-            total = total + gram_in[h, d]
-        result.append(total.reshape(half, width))
-    cross = jnp.transpose(result[1])[:half]
-    gram_ref[:half, :] = jnp.concatenate([result[0][:, :half], cross], axis=1)
-    gram_ref[half:, :] = result[1]
-    for copy in sent + passed + given + around:
+            total = total + gram_in[k, i]
+        gram_sum[k] = total
+        copy = remote(gram_sum.at[k], gram_far.at[k], h_send.at[k], h_recv.at[k], sibling)
+        copy.start()
+        last.append(copy)
+    for k, copy in enumerate(last):
+        copy.wait_recv()
+        total = gram_sum[k] + gram_far[k]
+        lower[(k + 1) * band:(k + 2) * band, :] = total
+        if k == 0:
+            lower[:band, :] = pltpu.roll(total, width - 2 * band, 1)
+    full = lower[...]
+    row = lax.broadcasted_iota(jnp.int32, (width, width), 0) // band
+    col = lax.broadcasted_iota(jnp.int32, (width, width), 1) // band
+    gram_ref[...] = jnp.where(col <= row, full, jnp.transpose(full))
+    for copy in sent + swaps + passed + given + around + last:
         copy.wait_send()
 
 
@@ -569,8 +602,9 @@
     n_grp, n_dev = lax.axis_size("grp"), lax.axis_size("dev")
     samples = sample_rows.shape[0]
     own = samples // (n_grp * n_dev)
-    n_z, peers = n_dev // 2, n_grp * 2
-    mine, picks, half = width // peers // 2, n_grp * LANES, width // 2
+    n_y, n_z, chips = n_grp // 2, n_dev // 2, n_grp
+    mine = 8
+    chunks, band, picks = width // (chips * mine), chips * mine, n_y * LANES
     f32, i32, bf16 = jnp.float32, jnp.int32, jnp.bfloat16
     dma = pltpu.SemaphoreType.DMA
     vmem = pl.BlockSpec(memory_space=pltpu.VMEM)
@@ -584,18 +618,24 @@
             pltpu.VMEM((rows // LANES, LANES), i32),
             pltpu.VMEM((samples // LANES, LANES), i32),
             pltpu.VMEM((width, rows), f32),
-            pltpu.VMEM((2, peers, mine, rows), f32),
-            pltpu.VMEM((n_z, rows, picks), bf16),
-            pltpu.VMEM((n_z, peers, 8, picks), f32),
-            pltpu.VMEM((2, n_z, mine, picks), f32),
-            pltpu.VMEM((2, n_z - 1, mine, picks), f32),
-            pltpu.VMEM((2, mine, picks), f32),
-            pltpu.VMEM((2, peers, mine, picks), f32),
+            pltpu.VMEM((chunks, chips, mine, rows), f32),
+            pltpu.VMEM((2, rows, n_z * picks), bf16),
+            pltpu.VMEM((2, chips, mine, n_z * picks), f32),
+            pltpu.VMEM((chunks, mine, n_z * picks), f32),
+            pltpu.VMEM((chunks, mine, n_z * picks), f32),
+            pltpu.VMEM((chunks, n_z, mine, picks), f32),
+            pltpu.VMEM((chunks, n_z - 1, mine, picks), f32),
+            pltpu.VMEM((chunks, mine, picks), f32),
+            pltpu.VMEM((chunks, chips, mine, picks), f32),
             pltpu.VMEM((LANES, width), f32),
-            pltpu.VMEM((2, half // 2, width), f32),
-            pltpu.VMEM((2, n_z, 2, half // 2, width), f32),
-            dma((3,)), dma((2, peers - 1)), dma((2, peers - 1)), dma((2, n_z - 1)), dma((2, n_z - 1)),
-            dma((2, peers - 1)), dma((2, peers - 1)), dma((2, 2 * n_z - 1)), dma((2, 2 * n_z - 1)),
+            pltpu.VMEM((chunks - 1, band, width), f32),
+            pltpu.VMEM((chunks - 1, n_z - 1, band, width), f32),
+            pltpu.VMEM((chunks - 1, band, width), f32),
+            pltpu.VMEM((chunks - 1, band, width), f32),
+            pltpu.VMEM((width, width), f32),
+            dma((3,)), dma((chunks, chips - 1)), dma((chunks, chips - 1)), dma((chunks,)), dma((chunks,)),
+            dma((chunks, n_z - 1)), dma((chunks, n_z - 1)), dma((chunks, chips - 1)), dma((chunks, chips - 1)),
+            dma((chunks - 1, n_z - 1)), dma((chunks - 1, n_z - 1)), dma((chunks - 1,)), dma((chunks - 1,)),
         ],
         compiler_params=pltpu.CompilerParams(collective_id=0, has_side_effects=True),
     )(
@@ -609,7 +649,7 @@
     rows, width = matrix.shape
     n_grp, n_dev = lax.axis_size("grp"), lax.axis_size("dev")
     paired = sample_rows.shape[0] * 2 == n_grp * n_dev * LANES
-    tiled = width == LANES and width % (n_grp * 2 * 16) == 0
+    tiled = width == LANES and width % (n_grp * 8) == 0 and width // (n_grp * 8) >= 3
     if paired and tiled and rows % LANES == 0:
         return plane_body(matrix, flip_bits, sample_rows)
     return general(matrix, flip_bits, sample_rows)

time: 28 us -> 27.1 us (0.968)
  Pallas kernels: 26 us -> 25 us
    pallas_call x1, Pallas kernels: 26 us -> 25 us  [plane_body(): pl.pallas_call(functools.partial(plane_kernel, n_grp, n_dev, rows, own),...]
where the time goes in v3:
time: 27.1 us; the launch traced here: 26.9 us
  Pallas kernels  25 us (92%)
  local copies, waits for them, and re-layouts  1.25 us (5%)
  between operations  0.64 us (2%)
    pallas_call x1, Pallas kernels, plane_body(): pl.pallas_call(functools.partial(plane_kernel, n_grp, n_dev, rows, own),...  25 us
    unnamed x2, local copies, waits for them, and re-layouts  1.25 us

profile of v3, /device:TPU:0, one launch (start us, length us, event | category | flops | bytes accessed | tf_op | source)
XLA Modules:
  0.0 26.9 jit_solution(5985788233356456372)
XLA Ops:
  0.6 25.0 %shard_map.50 = (f32[64,128]{1,0:T(8,128)S(1)}, f32[128,128]{1,0:T(8,128)S(1)}) custom-call(f32[512,128]{1,0:T(8,128)} %x_hbm.1, s32[4,128]{1,0:T(4,128)} %bitcast.3, s32[16,128]{1,0:T(8,128)} %bitcast.2), custom_call_target="tpu_custom_call" | custom-call | tf_op jit(solution)/shard_map/pallas_call | solution.py:611
  25.7 0.6 %copy.7 = f32[64,128]{1,0:T(8,128)} copy(f32[64,128]{1,0:T(8,128)S(1)} %get-tuple-element.2) | data formatting | bytes 65536
  26.3 0.6 %copy.8 = f32[128,128]{1,0:T(8,128)} copy(f32[128,128]{1,0:T(8,128)S(1)} %get-tuple-element.3) | data formatting | bytes 131072

commit v4 on v1

--- a/solution.py
+++ b/solution.py
@@ -353,7 +353,7 @@
     x_hbm, flip_hbm, sample_hbm, sketch_ref, gram_ref,
     x_ref, flip_ref, sample_ref, turned, slabs, signs, peer_signs, part, blocks, mixed, cols, turn_back,
     gpart, gslots, ghalf, gmine, gfull,
-    load_sem, in_send, in_recv, z_send, z_recv, out_send, out_recv, core_send, core_recv, gz_send, gz_recv,
+    load_sem, in_send, in_recv, z_send, z_recv, out_send, out_recv, core_send, core_recv, gz_send, gz_recv, far_recv,
 ):
     f32, bf16 = jnp.float32, jnp.bfloat16
     width = x_ref.shape[1]
@@ -377,11 +377,21 @@
         to_y, to_x, to_c = lax.rem(y + a, n_y), lax.rem(x + k, 2), lax.rem(core + b, 2)
         return to_y * 2 + to_c, to_x, to_c
 
+    far, first, final = [], 0, n_z - 1
+    for _ in range(n_z - 1):
+        down = z - first >= final - z
+        far.append(jnp.where(down, first, final))
+        first, final = first + jnp.where(down, 1, 0), final - jnp.where(down, 0, 1)
+    others = [lax.rem(z + d, n_z) for d in range(1, n_z)]
+
     def remote(src, dst, send, recv, grp, dev):
         return pltpu.make_async_remote_copy(
             src_ref=src, dst_ref=dst, send_sem=send, recv_sem=recv,
             device_id=(grp, dev), device_id_type=MESH,
         )
+
+    def arrival(slot, sem):
+        pltpu.make_async_copy(slot, slot, sem).wait()
 
     barrier = pltpu.get_barrier_semaphore()
     loads = [
@@ -419,10 +429,8 @@
         sent.append(copy)
     slabs[me] = turned[pl.ds(pl.multiple_of(me * mine, mine), mine), :]
 
-    order = sorted(range(n_z), key=lambda d: -min(d, n_z - d))
     low = lax.broadcasted_iota(jnp.int32, (16, LANES), 0)
-    for i, d in enumerate(order):
-        to_z = lax.rem(z + d, n_z)
+    for i, to_z in enumerate(far + [z]):
         for g in range(n_grp):
             wanted = sample_ref[pl.ds(g * span + to_z, 1), :]
             wide = jnp.broadcast_to(wanted, (16, LANES))
@@ -442,7 +450,7 @@
     high, mid = split2(slabs[...].reshape(peers * mine, rows))
     left = jnp.concatenate([high, mid], axis=0)
     passed = []
-    for i, d in enumerate(order):
+    for i, to_z in enumerate(far + [z]):
         product = jnp.dot(left, signs[i], preferred_element_type=f32)
         product = product[:peers * mine] + product[peers * mine:]
         total = None
@@ -450,17 +458,16 @@
             term = product[p * mine:(p + 1) * mine].reshape(mine // 8, 8, picks) * peer_signs[i, p][None]
             total = term if total is None else total + term
         part[i] = total.reshape(mine, picks)
-        if d:
+        if i < n_z - 1:
             copy = remote(
-                part.at[i], blocks.at[i], z_send.at[i], z_recv.at[i],
-                me_g, lax.rem(z + d, n_z) * 2 + x,
+                part.at[i], blocks.at[z], z_send.at[i], z_recv.at[z], me_g, to_z * 2 + x
             )
             copy.start()
             passed.append(copy)
     total = part[n_z - 1]
-    for i, copy in enumerate(passed):
-        copy.wait_recv()
-        total = total + blocks[i]
+    for from_z in others:
+        arrival(blocks.at[from_z], z_recv.at[from_z])
+        total = total + blocks[from_z]
     total = total * (1.0 / math.sqrt(rows * n_grp * n_dev))
     for c in range(2):
         mixed[c] = jnp.concatenate(
@@ -494,24 +501,36 @@
     sketch_ref[...] = turn_back[pl.ds(pl.multiple_of(x * own, own), own), :]
     swap.wait_recv()
     gmine[...] = gpart[core] + gslots[...]
-    around = []
-    for d in range(1, n_z):
-        copy = remote(
-            gmine, ghalf.at[d - 1], gz_send.at[d - 1], gz_recv.at[d - 1],
-            me_g, lax.rem(z + d, n_z) * 2 + x,
-        )
-        copy.start()
-        around.append(copy)
-    result = gmine[...]
-    for i, copy in enumerate(around):
-        copy.wait_recv()
-        result = result + ghalf[i]
-    gfull[core] = result
+    told = [
+        remote(gfull.at[core], gfull.at[core], gz_send.at[d - 1], far_recv.at[0], me_g, d * 2 + x)
+        for d in range(n_z - 1, 0, -1)
+    ]
     last = remote(gfull.at[core], gfull.at[core], core_send.at[1], core_recv.at[1], sibling, me_d)
-    last.start()
+    report = remote(gmine, ghalf.at[z], gz_send.at[0], gz_recv.at[z], me_g, x)
+
+    @pl.when(z == 0)
+    def _():
+        result = gmine[...]
+        for d in range(1, n_z):
+            arrival(ghalf.at[d], gz_recv.at[d])
+            result = result + ghalf[d]
+        gfull[core] = result
+        last.start()
+        for copy in told:
+            copy.start()
+        for copy in told:
+            copy.wait_send()
+
+    @pl.when(z > 0)
+    def _():
+        report.start()
+        arrival(gfull.at[core], far_recv.at[0])
+        last.start()
+        report.wait_send()
+
     last.wait_recv()
     gram_ref[...] = gfull[...].reshape(width, width)
-    for copy in sent + passed + given + around + [swap, last]:
+    for copy in sent + passed + given + [swap, last]:
         copy.wait_send()
 
 
@@ -587,17 +606,17 @@
             pltpu.VMEM((n_z, rows, picks), bf16),
             pltpu.VMEM((n_z, peers, 8, picks), f32),
             pltpu.VMEM((n_z, mine, picks), f32),
-            pltpu.VMEM((n_z - 1, mine, picks), f32),
+            pltpu.VMEM((n_z, mine, picks), f32),
             pltpu.VMEM((2, mine, n_y * LANES), f32),
             pltpu.VMEM((peers, mine, n_y * LANES), f32),
             pltpu.VMEM((LANES, width), f32),
             pltpu.VMEM((2, half, width), f32),
             pltpu.VMEM((half, width), f32),
-            pltpu.VMEM((n_z - 1, half, width), f32),
+            pltpu.VMEM((n_z, half, width), f32),
             pltpu.VMEM((half, width), f32),
             pltpu.VMEM((2, half, width), f32),
-            dma((3,)), dma((peers - 1,)), dma((peers - 1,)), dma((n_z - 1,)), dma((n_z - 1,)),
-            dma((peers - 1,)), dma((peers - 1,)), dma((2,)), dma((2,)), dma((n_z - 1,)), dma((n_z - 1,)),
+            dma((3,)), dma((peers - 1,)), dma((peers - 1,)), dma((n_z - 1,)), dma((n_z,)),
+            dma((peers - 1,)), dma((peers - 1,)), dma((2,)), dma((2,)), dma((n_z - 1,)), dma((n_z,)), dma((1,)),
         ],
         compiler_params=pltpu.CompilerParams(collective_id=0, has_side_effects=True),
     )(

time: 27 us -> 29.5 us (1.093)
  the two profiles are of different devices: /device:TPU:0 before, /device:TPU:9 now
where the time goes in v4:
time: 29.5 us; the launch traced here: 29.3 us
  Pallas kernels  27.4 us (93%)
  local copies, waits for them, and re-layouts  1.25 us (4%)
  between operations  0.64 us (2%)
    pallas_call x1, Pallas kernels, plane_body(): pl.pallas_call(functools.partial(plane_kernel, n_grp, n_dev, rows, own),...  27.4 us
    unnamed x2, local copies, waits for them, and re-layouts  1.25 us

profile of v4, /device:TPU:9, one launch (start us, length us, event | category | flops | bytes accessed | tf_op | source)
XLA Modules:
  0.0 29.3 jit_solution(6378722439531465667)
XLA Ops:
  0.6 27.4 %shard_map.50 = (f32[64,128]{1,0:T(8,128)S(1)}, f32[128,128]{1,0:T(8,128)S(1)}) custom-call(f32[512,128]{1,0:T(8,128)} %x_hbm.1, s32[4,128]{1,0:T(4,128)} %bitcast.3, s32[16,128]{1,0:T(8,128)} %bitcast.2), custom_call_target="tpu_custom_call" | custom-call | tf_op jit(solution)/shard_map/pallas_call | solution.py:595
  28.1 0.6 %copy.7 = f32[64,128]{1,0:T(8,128)} copy(f32[64,128]{1,0:T(8,128)S(1)} %get-tuple-element.2) | data formatting | bytes 65536
  28.7 0.6 %copy.8 = f32[128,128]{1,0:T(8,128)} copy(f32[128,128]{1,0:T(8,128)S(1)} %get-tuple-element.3) | data formatting | bytes 131072

commit v5 on v3

--- a/solution.py
+++ b/solution.py
@@ -352,9 +352,9 @@
     n_grp, n_dev, rows, own,
     x_hbm, flip_hbm, sample_hbm, sketch_ref, gram_ref,
     x_ref, flip_ref, sample_ref, turned, slabs, signs, peer_signs, lent, borrowed, part, blocks, mixed, cols,
-    turn_back, gram_out, gram_in, gram_sum, gram_far, lower,
+    turn_back, gram_out, gram_in, gram_sum, gram_far,
     load_sem, in_send, in_recv, c_send, c_recv, z_send, z_recv, out_send, out_recv,
-    g_send, g_recv, h_send, h_recv,
+    g_send, g_recv, h_send, h_recv, ready,
 ):
     f32, bf16 = jnp.float32, jnp.bfloat16
     width = x_ref.shape[1]
@@ -373,15 +373,23 @@
     me = y * 2 + x
 
     plane = [(a, k) for a in range(n_y - 1, -1, -1) for k in (1, 0) if a or k]
-    order = sorted(range(n_z), key=lambda d: -min(d, n_z - d))
+    far, first, final = [], 0, n_z - 1
+    for _ in range(n_z - 1):
+        down = z - first >= final - z
+        far.append(jnp.where(down, first, final))
+        first, final = first + jnp.where(down, 1, 0), final - jnp.where(down, 0, 1)
+    others = [lax.rem(z + d, n_z) for d in range(1, n_z)]
     sibling = (me_g + 1 - 2 * core, me_d)
 
     def across(a, k):
         to_y, to_x = lax.rem(y + a, n_y), lax.rem(x + k, 2)
         return (to_y * 2 + core, z * 2 + to_x), to_y * 2 + to_x
 
-    def along(d):
-        return me_g, lax.rem(z + d, n_z) * 2 + x
+    def along(to_z):
+        return me_g, to_z * 2 + x
+
+    def arrival(slot, sem):
+        pltpu.make_async_copy(slot, slot, sem).wait()
 
     def remote(src, dst, send, recv, at):
         return pltpu.make_async_remote_copy(
@@ -398,9 +406,13 @@
     ]
     for copy in loads:
         copy.start()
-    greeted = [across(*at)[0] for at in plane] + [along(d) for d in order[:-1]] + [sibling]
+    greeted = [across(*at)[0] for at in plane] + [sibling]
     for at in greeted:
         pl.semaphore_signal(barrier, inc=1, device_id=at, device_id_type=MESH)
+    for step in range(1, n_z):
+        @pl.when(z + step < n_z)
+        def _():
+            pl.semaphore_signal(barrier, inc=1, device_id=along(z + step), device_id_type=MESH)
     for copy in loads:
         copy.wait()
 
@@ -408,10 +420,11 @@
     for k in range(rows // LANES):
         at = slice(k * LANES, (k + 1) * LANES)
         turned[:, at] = jnp.transpose(x_ref[at, :]) * toggles[k:k + 1, :]
-    pl.semaphore_wait(barrier, len(greeted))
+    pl.semaphore_wait(barrier, len(greeted) + z)
 
     sent, swaps, passed, given, around, last = [], [], [], [], [], []
-    for k in range(chunks):
+    low = lax.broadcasted_iota(jnp.int32, (16, LANES), 0)
+    for k in range(2):
         for m, at in enumerate(plane):
             to, chip = across(*at)
             copy = remote(
@@ -420,14 +433,14 @@
             )
             copy.start()
             sent.append(copy)
-    for k in range(chunks):
         slabs[k, me] = turned[pl.ds(pl.multiple_of(k * band + me * mine, mine), mine), :]
-
-    low = lax.broadcasted_iota(jnp.int32, (16, LANES), 0)
-    for r in range(2):
-        owner = core if r else 1 - core
-        for i, d in enumerate(order):
-            to_z = lax.rem(z + d, n_z)
+        if k == 0:
+            for step in range(1, n_z):
+                @pl.when(z >= step)
+                def _():
+                    pl.semaphore_signal(ready, inc=1, device_id=along(z - step), device_id_type=MESH)
+        owner = core if k else 1 - core
+        for i, to_z in enumerate(far + [z]):
             for j in range(n_y):
                 at = slice(i * picks + j * LANES, i * picks + (j + 1) * LANES)
                 wanted = sample_ref[pl.ds((j * 2 + owner) * span + to_z, 1), :]
@@ -436,12 +449,12 @@
                 for bit in range(4, row_bits):
                     factor = (1 - 2 * ((wide >> bit) & 1)).astype(f32).astype(bf16)
                     pieces += [piece * factor for piece in pieces]
-                for k, piece in enumerate(pieces):
-                    signs[r, k * 16:(k + 1) * 16, at] = piece
+                for r, piece in enumerate(pieces):
+                    signs[k, r * 16:(r + 1) * 16, at] = piece
                 wide = wide[:8]
                 for q in range(chips):
                     holder = ((q // 2 * 2 + core) * n_dev + z * 2 + q % 2) * rows
-                    peer_signs[r, q, :, at] = sign_of(wide & holder, all_bits)
+                    peer_signs[k, q, :, at] = sign_of(wide & holder, all_bits)
 
     def halves(k):
         high, mid = split2(slabs[k].reshape(band, rows))
@@ -452,18 +465,18 @@
         product = product[:band] + product[band:]
         total = None
         for q in range(chips):
-            term = product[q * mine:(q + 1) * mine] * peer_signs[r, q]
+            term = product[q * mine:(q + 1) * mine].reshape(mine // 8, 8, n_z * picks) * peer_signs[r, q][None]
             total = term if total is None else total + term
-        return total
+        return total.reshape(mine, n_z * picks)
 
     def settle(k):
         swaps[k].wait_recv()
-        for i, d in enumerate(order):
+        for i, to_z in enumerate(far + [z]):
             at = slice(i * picks, (i + 1) * picks)
             part[k, i] = part[k, i] + borrowed[k, :, at]
-            if d:
+            if i < n_z - 1:
                 copy = remote(
-                    part.at[k, i], blocks.at[k, i], z_send.at[k, i], z_recv.at[k, i], along(d)
+                    part.at[k, i], blocks.at[k, z], z_send.at[k, i], z_recv.at[k, z], along(to_z)
                 )
                 copy.start()
                 passed.append(copy)
@@ -476,7 +489,11 @@
         copy = remote(lent.at[k], borrowed.at[k], c_send.at[k], c_recv.at[k], sibling)
         copy.start()
         swaps.append(copy)
-        if k:
+        if k == 0:
+            @pl.when(z < n_z - 1)
+            def _():
+                pl.semaphore_wait(ready, n_z - 1 - z)
+        else:
             settle(k - 1)
         mixture = partial(left, 1)
         for i in range(n_z):
@@ -484,9 +501,9 @@
     settle(chunks - 1)
     for k in range(chunks):
         total = part[k, n_z - 1]
-        for i, copy in enumerate(passed[k * (n_z - 1):(k + 1) * (n_z - 1)]):
-            copy.wait_recv()
-            total = total + blocks[k, i]
+        for from_z in others:
+            arrival(blocks.at[k, from_z], z_recv.at[k, from_z])
+            total = total + blocks[k, from_z]
         mixed[k] = total * (1.0 / math.sqrt(rows * n_grp * n_dev))
         for m, at in enumerate(plane):
             copy = remote(
@@ -496,7 +513,8 @@
             given.append(copy)
         cols[k, me] = mixed[k]
 
-    right, held = None, None
+    right = None
+    areas = [slice(0, band // 2), slice(band // 2, band // 2 + band)]
     for k in range(chunks):
         for copy in given[k * len(plane):(k + 1) * len(plane)]:
             copy.wait_recv()
@@ -508,17 +526,11 @@
             (((1,), (1,)), ((), ())), preferred_element_type=f32,
         ) * (1.0 / samples)
         if k == 0:
-            held = gram
-            continue
-        if k == 1:
-            gram = jnp.concatenate([gram, held], axis=1)
-        room = width - gram.shape[1]
-        if room:
-            gram = jnp.concatenate([gram, jnp.zeros((band, room), f32)], axis=1)
-        gram_out[k - 1] = gram
-        for i, d in enumerate(order[:-1]):
+            gram = jnp.concatenate([gram[:band // 2], gram[band // 2:]], axis=1)
+        gram_out[areas[k]] = gram
+        for i, to_z in enumerate(far):
             copy = remote(
-                gram_out.at[k - 1], gram_in.at[k - 1, i], g_send.at[k - 1, i], g_recv.at[k - 1, i], along(d)
+                gram_out.at[areas[k]], gram_in.at[z, areas[k]], g_send.at[k, i], g_recv.at[k, z], along(to_z)
             )
             copy.start()
             around.append(copy)
@@ -526,25 +538,22 @@
     block = cols[:, :, :, pl.ds(pl.multiple_of(y * LANES, LANES), LANES)].reshape(width, LANES)
     turn_back[...] = jnp.transpose(block)
     sketch_ref[...] = turn_back[pl.ds(pl.multiple_of(x * own, own), own), :]
-    for k in range(chunks - 1):
-        total = gram_out[k]
-        for i, copy in enumerate(around[k * (n_z - 1):(k + 1) * (n_z - 1)]):
-            copy.wait_recv()
-            total = total + gram_in[k, i]
-        gram_sum[k] = total
-        copy = remote(gram_sum.at[k], gram_far.at[k], h_send.at[k], h_recv.at[k], sibling)
+    for k in range(chunks):
+        total = gram_out[areas[k]]
+        for from_z in others:
+            arrival(gram_in.at[from_z, areas[k]], g_recv.at[k, from_z])
+            total = total + gram_in[from_z, areas[k]]
+        gram_sum[areas[k]] = total
+        copy = remote(gram_sum.at[areas[k]], gram_far.at[areas[k]], h_send.at[k], h_recv.at[k], sibling)
         copy.start()
         last.append(copy)
-    for k, copy in enumerate(last):
+    for copy in last:
         copy.wait_recv()
-        total = gram_sum[k] + gram_far[k]
-        lower[(k + 1) * band:(k + 2) * band, :] = total
-        if k == 0:
-            lower[:band, :] = pltpu.roll(total, width - 2 * band, 1)
-    full = lower[...]
-    row = lax.broadcasted_iota(jnp.int32, (width, width), 0) // band
-    col = lax.broadcasted_iota(jnp.int32, (width, width), 1) // band
-    gram_ref[...] = jnp.where(col <= row, full, jnp.transpose(full))
+    early, late = (gram_sum[at] + gram_far[at] for at in areas)
+    early = jnp.concatenate([early[:, :band], early[:, band:]], axis=0)
+    cross = jnp.transpose(late)[:band]
+    gram_ref[:band, :] = jnp.concatenate([early, cross], axis=1)
+    gram_ref[band:, :] = late
     for copy in sent + swaps + passed + given + around + last:
         copy.wait_send()
 
@@ -603,8 +612,8 @@
     samples = sample_rows.shape[0]
     own = samples // (n_grp * n_dev)
     n_y, n_z, chips = n_grp // 2, n_dev // 2, n_grp
-    mine = 8
-    chunks, band, picks = width // (chips * mine), chips * mine, n_y * LANES
+    chunks = 2
+    mine, band, picks = width // (chips * chunks), width // chunks, n_y * LANES
     f32, i32, bf16 = jnp.float32, jnp.int32, jnp.bfloat16
     dma = pltpu.SemaphoreType.DMA
     vmem = pl.BlockSpec(memory_space=pltpu.VMEM)
@@ -620,22 +629,22 @@
             pltpu.VMEM((width, rows), f32),
             pltpu.VMEM((chunks, chips, mine, rows), f32),
             pltpu.VMEM((2, rows, n_z * picks), bf16),
-            pltpu.VMEM((2, chips, mine, n_z * picks), f32),
+            pltpu.VMEM((2, chips, 8, n_z * picks), f32),
             pltpu.VMEM((chunks, mine, n_z * picks), f32),
             pltpu.VMEM((chunks, mine, n_z * picks), f32),
             pltpu.VMEM((chunks, n_z, mine, picks), f32),
-            pltpu.VMEM((chunks, n_z - 1, mine, picks), f32),
+            pltpu.VMEM((chunks, n_z, mine, picks), f32),
             pltpu.VMEM((chunks, mine, picks), f32),
             pltpu.VMEM((chunks, chips, mine, picks), f32),
             pltpu.VMEM((LANES, width), f32),
-            pltpu.VMEM((chunks - 1, band, width), f32),
-            pltpu.VMEM((chunks - 1, n_z - 1, band, width), f32),
-            pltpu.VMEM((chunks - 1, band, width), f32),
-            pltpu.VMEM((chunks - 1, band, width), f32),
-            pltpu.VMEM((width, width), f32),
+            pltpu.VMEM((band // 2 + band, width), f32),
+            pltpu.VMEM((n_z, band // 2 + band, width), f32),
+            pltpu.VMEM((band // 2 + band, width), f32),
+            pltpu.VMEM((band // 2 + band, width), f32),
             dma((3,)), dma((chunks, chips - 1)), dma((chunks, chips - 1)), dma((chunks,)), dma((chunks,)),
-            dma((chunks, n_z - 1)), dma((chunks, n_z - 1)), dma((chunks, chips - 1)), dma((chunks, chips - 1)),
-            dma((chunks - 1, n_z - 1)), dma((chunks - 1, n_z - 1)), dma((chunks - 1,)), dma((chunks - 1,)),
+            dma((chunks, n_z - 1)), dma((chunks, n_z)), dma((chunks, chips - 1)), dma((chunks, chips - 1)),
+            dma((chunks, n_z - 1)), dma((chunks, n_z)), dma((chunks,)), dma((chunks,)),
+            pltpu.SemaphoreType.REGULAR,
         ],
         compiler_params=pltpu.CompilerParams(collective_id=0, has_side_effects=True),
     )(
@@ -649,7 +658,7 @@
     rows, width = matrix.shape
     n_grp, n_dev = lax.axis_size("grp"), lax.axis_size("dev")
     paired = sample_rows.shape[0] * 2 == n_grp * n_dev * LANES
-    tiled = width == LANES and width % (n_grp * 8) == 0 and width // (n_grp * 8) >= 3
+    tiled = width == LANES and width % (n_grp * 16) == 0
     if paired and tiled and rows % LANES == 0:
         return plane_body(matrix, flip_bits, sample_rows)
     return general(matrix, flip_bits, sample_rows)

time: 27.1 us -> 26.6 us (0.982)
  Pallas kernels: 25 us -> 24.5 us
    pallas_call x1, Pallas kernels: 25 us -> 24.5 us  [plane_body(): pl.pallas_call(functools.partial(plane_kernel, n_grp, n_dev, rows, own),...]
where the time goes in v5:
time: 26.6 us; the launch traced here: 26.4 us
  Pallas kernels  24.5 us (92%)
  local copies, waits for them, and re-layouts  1.25 us (5%)
  between operations  0.64 us (2%)
    pallas_call x1, Pallas kernels, plane_body(): pl.pallas_call(functools.partial(plane_kernel, n_grp, n_dev, rows, own),...  24.5 us
    unnamed x2, local copies, waits for them, and re-layouts  1.25 us

profile of v5, /device:TPU:0, one launch (start us, length us, event | category | flops | bytes accessed | tf_op | source)
XLA Modules:
  0.0 26.4 jit_solution(4059445340942509023)
XLA Ops:
  0.6 24.5 %shard_map.50 = (f32[64,128]{1,0:T(8,128)S(1)}, f32[128,128]{1,0:T(8,128)S(1)}) custom-call(f32[512,128]{1,0:T(8,128)} %x_hbm.1, s32[4,128]{1,0:T(4,128)} %bitcast.3, s32[16,128]{1,0:T(8,128)} %bitcast.2), custom_call_target="tpu_custom_call" | custom-call | tf_op jit(solution)/shard_map/pallas_call | solution.py:620
  25.2 0.6 %copy.7 = f32[64,128]{1,0:T(8,128)} copy(f32[64,128]{1,0:T(8,128)S(1)} %get-tuple-element.2) | data formatting | bytes 65536
  25.8 0.6 %copy.8 = f32[128,128]{1,0:T(8,128)} copy(f32[128,128]{1,0:T(8,128)S(1)} %get-tuple-element.3) | data formatting | bytes 131072

commit v6 on v5

--- a/solution.py
+++ b/solution.py
@@ -352,9 +352,9 @@
     n_grp, n_dev, rows, own,
     x_hbm, flip_hbm, sample_hbm, sketch_ref, gram_ref,
     x_ref, flip_ref, sample_ref, turned, slabs, signs, peer_signs, lent, borrowed, part, blocks, mixed, cols,
-    turn_back, gram_out, gram_in, gram_sum, gram_far,
+    turn_back, gram_part, gram_sib, gram_out, gram_in, gram_full,
     load_sem, in_send, in_recv, c_send, c_recv, z_send, z_recv, out_send, out_recv,
-    g_send, g_recv, h_send, h_recv, ready,
+    s_send, s_recv, g_send, g_recv, h_send, h_recv, ready,
 ):
     f32, bf16 = jnp.float32, jnp.bfloat16
     width = x_ref.shape[1]
@@ -514,10 +514,24 @@
         cols[k, me] = mixed[k]
 
     right = None
-    areas = [slice(0, band // 2), slice(band // 2, band // 2 + band)]
+    areas = [slice(0, band // 4), slice(band // 4, band // 4 + band // 2)]
+
+    def spread(k):
+        halves_in[k].wait_recv()
+        gram_out[areas[k]] = gram_part[core, areas[k]] + gram_sib[areas[k]]
+        for i, to_z in enumerate(far):
+            copy = remote(
+                gram_out.at[areas[k]], gram_in.at[z, areas[k]], g_send.at[k, i], g_recv.at[k, z], along(to_z)
+            )
+            copy.start()
+            around.append(copy)
+
+    halves_in = []
     for k in range(chunks):
         for copy in given[k * len(plane):(k + 1) * len(plane)]:
             copy.wait_recv()
+        if k:
+            spread(k - 1)
         high, mid = split2(cols[k].reshape(band, picks))
         fresh = jnp.concatenate([high, high, mid], axis=1)
         right = fresh if right is None else jnp.concatenate([right, fresh], axis=0)
@@ -526,35 +540,38 @@
             (((1,), (1,)), ((), ())), preferred_element_type=f32,
         ) * (1.0 / samples)
         if k == 0:
-            gram = jnp.concatenate([gram[:band // 2], gram[band // 2:]], axis=1)
-        gram_out[areas[k]] = gram
-        for i, to_z in enumerate(far):
-            copy = remote(
-                gram_out.at[areas[k]], gram_in.at[z, areas[k]], g_send.at[k, i], g_recv.at[k, z], along(to_z)
-            )
-            copy.start()
-            around.append(copy)
+            gram = gram.reshape(2, 2, band // 4, band)
+            gram = jnp.concatenate([gram[:, 0], gram[:, 1]], axis=2)
+        gram_part[:, areas[k]] = gram.reshape(2, -1, width)
+        copy = remote(
+            gram_part.at[1 - core, areas[k]], gram_sib.at[areas[k]], s_send.at[k], s_recv.at[k], sibling
+        )
+        copy.start()
+        halves_in.append(copy)
 
     block = cols[:, :, :, pl.ds(pl.multiple_of(y * LANES, LANES), LANES)].reshape(width, LANES)
     turn_back[...] = jnp.transpose(block)
     sketch_ref[...] = turn_back[pl.ds(pl.multiple_of(x * own, own), own), :]
+    spread(chunks - 1)
     for k in range(chunks):
         total = gram_out[areas[k]]
         for from_z in others:
             arrival(gram_in.at[from_z, areas[k]], g_recv.at[k, from_z])
             total = total + gram_in[from_z, areas[k]]
-        gram_sum[areas[k]] = total
-        copy = remote(gram_sum.at[areas[k]], gram_far.at[areas[k]], h_send.at[k], h_recv.at[k], sibling)
+        gram_full[core, areas[k]] = total
+        here = gram_full.at[core, areas[k]]
+        copy = remote(here, here, h_send.at[k], h_recv.at[k], sibling)
         copy.start()
         last.append(copy)
     for copy in last:
         copy.wait_recv()
-    early, late = (gram_sum[at] + gram_far[at] for at in areas)
-    early = jnp.concatenate([early[:, :band], early[:, band:]], axis=0)
+    early, late = (gram_full[:, at] for at in areas)
+    early = jnp.stack([early[:, :, :band], early[:, :, band:]], axis=1).reshape(band, band)
+    late = late.reshape(band, width)
     cross = jnp.transpose(late)[:band]
     gram_ref[:band, :] = jnp.concatenate([early, cross], axis=1)
     gram_ref[band:, :] = late
-    for copy in sent + swaps + passed + given + around + last:
+    for copy in sent + swaps + passed + given + halves_in + around + last:
         copy.wait_send()
 
 
@@ -606,6 +623,17 @@
     )
 
 
+def write_out(sketch_in, gram_in, sketch_ref, gram_ref, sem):
+    copies = [
+        pltpu.make_async_copy(gram_in, gram_ref, sem.at[0]),
+        pltpu.make_async_copy(sketch_in, sketch_ref, sem.at[1]),
+    ]
+    for copy in copies:
+        copy.start()
+    for copy in copies:
+        copy.wait()
+
+
 def plane_body(matrix, flip_bits, sample_rows):
     rows, width = matrix.shape
     n_grp, n_dev = lax.axis_size("grp"), lax.axis_size("dev")
@@ -617,7 +645,7 @@
     f32, i32, bf16 = jnp.float32, jnp.int32, jnp.bfloat16
     dma = pltpu.SemaphoreType.DMA
     vmem = pl.BlockSpec(memory_space=pltpu.VMEM)
-    return pl.pallas_call(
+    sketch, gram = pl.pallas_call(
         functools.partial(plane_kernel, n_grp, n_dev, rows, own),
         out_shape=(pltpu.VMEM((own, width), f32), pltpu.VMEM((width, width), f32)),
         in_specs=[pl.BlockSpec(memory_space=pl.ANY)] * 3,
@@ -637,13 +665,14 @@
             pltpu.VMEM((chunks, mine, picks), f32),
             pltpu.VMEM((chunks, chips, mine, picks), f32),
             pltpu.VMEM((LANES, width), f32),
-            pltpu.VMEM((band // 2 + band, width), f32),
-            pltpu.VMEM((n_z, band // 2 + band, width), f32),
-            pltpu.VMEM((band // 2 + band, width), f32),
-            pltpu.VMEM((band // 2 + band, width), f32),
+            pltpu.VMEM((2, band * 3 // 4, width), f32),
+            pltpu.VMEM((band * 3 // 4, width), f32),
+            pltpu.VMEM((band * 3 // 4, width), f32),
+            pltpu.VMEM((n_z, band * 3 // 4, width), f32),
+            pltpu.VMEM((2, band * 3 // 4, width), f32),
             dma((3,)), dma((chunks, chips - 1)), dma((chunks, chips - 1)), dma((chunks,)), dma((chunks,)),
             dma((chunks, n_z - 1)), dma((chunks, n_z)), dma((chunks, chips - 1)), dma((chunks, chips - 1)),
-            dma((chunks, n_z - 1)), dma((chunks, n_z)), dma((chunks,)), dma((chunks,)),
+            dma((chunks,)), dma((chunks,)), dma((chunks, n_z - 1)), dma((chunks, n_z)), dma((chunks,)), dma((chunks,)),
             pltpu.SemaphoreType.REGULAR,
         ],
         compiler_params=pltpu.CompilerParams(collective_id=0, has_side_effects=True),
@@ -652,6 +681,17 @@
         flip_bits.reshape(rows // LANES, LANES),
         sample_rows.reshape(samples // LANES, LANES),
     )
+    hbm = pl.BlockSpec(memory_space=pl.ANY)
+    return pl.pallas_call(
+        write_out,
+        out_shape=(jax.ShapeDtypeStruct((own, width), f32), jax.ShapeDtypeStruct((width, width), f32)),
+        in_specs=[vmem, vmem],
+        out_specs=(hbm, hbm),
+        scratch_shapes=[dma((2,))],
+    )(
+        pltpu.with_memory_space_constraint(sketch, pltpu.VMEM),
+        pltpu.with_memory_space_constraint(gram, pltpu.VMEM),
+    )
 
 
 def body(matrix, flip_bits, sample_rows):

time: 26.6 us -> 25.9 us (0.974)
  local copies, waits for them, and re-layouts: 1.25 us -> 0 us
  Pallas kernels: 24.5 us -> 25.1 us
    unnamed x2 -> x0, local copies, waits for them, and re-layouts: 1.25 us -> none
    pallas_call x0 -> x1, Pallas kernels: none -> 0.66 us  [plane_body(): pl.pallas_call(write_out, out_shape=(jax.ShapeDtypeStruct((own, width), f...]
where the time goes in v6:
time: 25.9 us; the launch traced here: 25.7 us
  Pallas kernels  25.1 us (97%)
  between operations  0.64 us (2%)
    pallas_call x1, Pallas kernels, plane_body(): pl.pallas_call(functools.partial(plane_kernel, n_grp, n_dev, rows, own),...  24.4 us
    pallas_call x1, Pallas kernels, plane_body(): pl.pallas_call(write_out, out_shape=(jax.ShapeDtypeStruct((own, width), f...  0.66 us

profile of v6, /device:TPU:0, one launch (start us, length us, event | category | flops | bytes accessed | tf_op | source)
XLA Modules:
  0.0 25.7 jit_solution(18029130190889768071)
XLA Ops:
  0.6 24.4 %shard_map.50 = (f32[64,128]{1,0:T(8,128)S(1)}, f32[128,128]{1,0:T(8,128)S(1)}) custom-call(f32[512,128]{1,0:T(8,128)} %x_hbm.1, s32[4,128]{1,0:T(4,128)} %bitcast.3, s32[16,128]{1,0:T(8,128)} %bitcast.2), custom_call_target="tpu_custom_call" | custom-call | tf_op jit(solution)/shard_map/pallas_call | solution.py:648
  25.1 0.7 %shard_map.51 = (f32[64,128]{1,0:T(8,128)}, f32[128,128]{1,0:T(8,128)}) custom-call(f32[64,128]{1,0:T(8,128)S(1)} %get-tuple-element.4.sketch_in, f32[128,128]{1,0:T(8,128)S(1)} %get-tuple-element.5.gram_in), custom_call_target="tpu_custom_call" | custom-call | tf_op jit(solution)/shard_map/pallas_call | solution.py:685
